TPU v7x, 32 devices: a whole 2x2x4 slice. The times are simulated.
32 devices in a mesh: wide: 8 (over z, y), narrow: 4 (over x, core).
Axes of the slice: x: 2, y: 2, z: 4, core: 2. Of those that a mesh axis runs over, the one named last changes fastest.
Arguments:
- solution: float32 [8, 16384], P(None, ('wide', 'narrow')), may hold values from -6 to 6
- residual: float32 [8, 16384], P(None, ('wide', 'narrow')), may hold values from -600 to 600
- direction: float32 [8, 16384], P(None, ('wide', 'narrow')), may hold values from -600 to 600
- error_var: float32 [16384], P(('wide', 'narrow')), may hold values from 0.25 to 2
- footprint: bfloat16 [16384, 4, 128], P(('wide', 'narrow')), may hold values from -0.25 to 0.25
- tiles: int32 [16384, 4], P(('wide', 'narrow')), may hold values from 0 to 1279
- window: int32 [16384, 1], P(('wide', 'narrow')), may hold values from 0 to 7; in each aligned block of 512 rows (0 to 511, 512 to 1023, ...) at most 160 rows name the same one
- temporal: bfloat16 [320, 320], replicated, may hold values from -40 to 40, as said below
- spatial_lat: bfloat16 [128, 128], replicated, may hold values from -40 to 40, as said below
- spatial_lon: bfloat16 [128, 128], replicated, may hold values from -40 to 40, as said below
Outputs:
- solution_new: float32 [8, 16384], P(None, ('wide', 'narrow'))
- residual_new: float32 [8, 16384], P(None, ('wide', 'narrow'))
- direction_new: float32 [8, 16384], P(None, ('wide', 'narrow'))
Inputs may be any that keep to these rules, and one draw needn't show every extreme that they name: At most 160 of the observations held by one device share a window, and some device reaches that in every draw. `temporal`: A symmetric positive definite covariance. `spatial_lat`: A symmetric positive definite covariance. `spatial_lon`: A symmetric positive definite covariance.
All inputs are finite; a program needn't handle non-finite values.
Results may differ from a plain program's by a relative error of at most 0.004.
Values may be sent and summed in bfloat16 or wider, within the bound.
A program may use at most 128 MiB of HBM per device.

v0:
```python
import math
import jax
import jax.numpy as jnp
from jax import lax
from jax.sharding import PartitionSpec as P

HIGHEST = lax.Precision.HIGHEST


def chol_solve(matrix, right):
    chol_low = jnp.linalg.cholesky(matrix)
    half_solve = lax.linalg.triangular_solve(chol_low, right, left_side=True, lower=True)
    return lax.linalg.triangular_solve(
        chol_low, half_solve, left_side=True, lower=True, transpose_a=True
    )


def gram_matrix(left, right):
    return jnp.dot(left, right.T, precision=HIGHEST)


def on_device(
    solution,
    residual,
    direction,
    error_var,
    footprint,
    tiles,
    window,
    temporal,
    spatial_lat,
    spatial_lon,
):
    n_wide = lax.axis_size("wide")
    n_narrow = lax.axis_size("narrow")
    rhs_count, obs_dev = direction.shape
    days_total = temporal.shape[0]
    day_dev = days_total // n_wide
    lat_total = spatial_lat.shape[0]
    lat_band = lat_total // n_narrow
    lon_count = spatial_lon.shape[0]
    tile_count = tiles.shape[1]
    capacity = obs_dev * 5 // (2 * n_wide)
    slot_total = n_wide * capacity
    tiles_local = day_dev * lat_band
    window_id = window[:, 0]
    dir_half = direction.astype(jnp.bfloat16)
    matches = (window_id[:, None] == jnp.arange(n_wide, dtype=jnp.int32)[None, :]).astype(jnp.int32)
    before = jnp.cumsum(matches, axis=0) - matches
    position = jnp.sum(before * matches, axis=1)
    slot_index = window_id * capacity + position
    source = (
        jnp.full((slot_total,), obs_dev, jnp.int32)
        .at[slot_index]
        .set(jnp.arange(obs_dev, dtype=jnp.int32))
    )
    foot_rows = jnp.concatenate(
        [
            footprint.reshape(obs_dev, tile_count * lon_count),
            jnp.zeros((1, tile_count * lon_count), jnp.bfloat16),
        ],
        0,
    )
    dir_rows = jnp.concatenate([dir_half.T, jnp.zeros((1, rhs_count), jnp.bfloat16)], 0)
    tile_rows = jnp.concatenate([tiles, jnp.zeros((1, tile_count), jnp.int32)], 0)
    recv_foot, recv_dir, recv_tiles = (
        lax.all_to_all(
            foot_rows[source].reshape(n_wide, capacity, tile_count * lon_count),
            "wide",
            split_axis=0,
            concat_axis=0,
            tiled=True,
        ),
        lax.all_to_all(
            dir_rows[source].reshape(n_wide, capacity, rhs_count),
            "wide",
            split_axis=0,
            concat_axis=0,
            tiled=True,
        ),
        lax.all_to_all(
            tile_rows[source].reshape(n_wide, capacity, tile_count),
            "wide",
            split_axis=0,
            concat_axis=0,
            tiled=True,
        ),
    )
    block_size = math.gcd(slot_total, 128)
    block_count = slot_total // block_size
    rows_block = block_size * tile_count
    foot_blocks = recv_foot.reshape(block_count, rows_block, lon_count)
    dir_blocks = jnp.repeat(recv_dir.reshape(slot_total, rhs_count), tile_count, axis=0).reshape(
        block_count, rows_block, rhs_count
    )
    id_blocks = recv_tiles.reshape(block_count, rows_block)
    tile_range = jnp.arange(tiles_local, dtype=jnp.int32)

    def adjoint_step(accum, inputs):
        foot_block, dir_block, id_block = inputs
        onehot = (id_block[None, :] == tile_range[:, None]).astype(jnp.bfloat16)
        weighted = (onehot[:, None, :] * dir_block.T[None, :, :]).reshape(
            tiles_local * rhs_count, rows_block
        )
        return (accum + jnp.dot(weighted, foot_block, preferred_element_type=jnp.float32), None)

    start_accum = jnp.zeros((tiles_local * rhs_count, lon_count), jnp.float32)
    accum, _ = lax.scan(adjoint_step, start_accum, (foot_blocks, dir_blocks, id_blocks))
    flat_flux = accum.astype(jnp.bfloat16).reshape(day_dev, lat_band * rhs_count * lon_count)
    all_days = lax.all_to_all(flat_flux, "wide", split_axis=1, concat_axis=0, tiled=True)
    mixed_days = jnp.dot(temporal, all_days, preferred_element_type=jnp.float32).astype(
        jnp.bfloat16
    )
    timed_flux = lax.all_to_all(mixed_days, "wide", split_axis=0, concat_axis=1, tiled=True)
    timed_flux = timed_flux.reshape(day_dev, lat_band, rhs_count, lon_count)
    narrow_index = lax.axis_index("narrow")
    lat_rows = lax.dynamic_slice_in_dim(spatial_lat, narrow_index * lat_band, lat_band, 0)
    lat_sum = jnp.einsum(
        "ab,dbrl->darl",
        lat_rows,
        lax.all_gather(timed_flux, "narrow", axis=1, tiled=True),
        preferred_element_type=jnp.float32,
    )
    spread_lat = lat_sum.astype(jnp.bfloat16)
    smoothed = jnp.dot(
        spread_lat.reshape(-1, lon_count), spatial_lon.T, preferred_element_type=jnp.float32
    ).astype(jnp.bfloat16)
    flux_table = smoothed.reshape(tiles_local, rhs_count * lon_count)

    def forward_step(accum_dummy, inputs):
        foot_block, id_block = inputs
        picked = flux_table[id_block].reshape(rows_block, rhs_count, lon_count)
        return (
            accum_dummy,
            jnp.einsum("jrl,jl->jr", picked, foot_block, preferred_element_type=jnp.float32),
        )

    _, model_rows = lax.scan(forward_step, jnp.zeros((), jnp.float32), (foot_blocks, id_blocks))
    back_rows = (
        model_rows.reshape(slot_total, tile_count, rhs_count)
        .sum(axis=1)
        .reshape(n_wide, capacity, rhs_count)
    )
    home_rows = lax.all_to_all(back_rows, "wide", split_axis=0, concat_axis=0, tiled=True).reshape(
        slot_total, rhs_count
    )
    model_part = home_rows[slot_index].T
    model_image = model_part + error_var[None, :] * direction
    curvature, res_norm = lax.psum(
        (gram_matrix(direction, model_image), gram_matrix(residual, residual)), ("wide", "narrow")
    )
    sym = 0.5 * (curvature + curvature.T)
    step_matrix = chol_solve(sym, res_norm)
    residual_new = residual - jnp.dot(step_matrix.T, model_image, precision=HIGHEST)
    norm_new = lax.psum(gram_matrix(residual_new, residual_new), ("wide", "narrow"))
    solution_new = solution + jnp.dot(step_matrix.T, direction, precision=HIGHEST)
    ratio_matrix = chol_solve(res_norm, norm_new)
    direction_new = residual_new + jnp.dot(ratio_matrix.T, direction, precision=HIGHEST)
    return (solution_new, residual_new, direction_new)


def solution(mesh):
    in_specs = (
        P(None, ("wide", "narrow")),
        P(None, ("wide", "narrow")),
        P(None, ("wide", "narrow")),
        P(("wide", "narrow")),
        P(("wide", "narrow"), None, None),
        P(("wide", "narrow"), None),
        P(("wide", "narrow"), None),
        P(),
        P(),
        P(),
    )
    out_specs = (
        P(None, ("wide", "narrow")),
        P(None, ("wide", "narrow")),
        P(None, ("wide", "narrow")),
    )
    return jax.shard_map(
        on_device, mesh=mesh, in_specs=in_specs, out_specs=out_specs, check_vma=False
    )
```

profile of v0, /device:TPU:0, one launch (start us, length us, event | category | flops | bytes accessed | tf_op | source)
XLA Modules:
  0.0 548.3 jit_solution(6296830245109133020)
XLA Ops:
  11.3 2.4 scatter_custom_fusion
  14.7 2.4 gather_fusion.1
  18.0 7.3 %all-to-all-start = ((s32[8,160,4]{1,2,0:T(4,128)}), s32[8,160,4]{1,2,0:T(4,128)S(1)}, u32[]{:S(2)}, u32[]{:S(2)}) async-start(s32[8,160,4]{1,2,0:T(4,128)} %copy.140), calls=%async_computation | async-start | bytes 65536 | tf_op jit(solution)/shard_map/all_to_all | solution.py:81
  25.5 2.8 gather_fusion.2
  29.2 2.9 all-to-all-done
  32.0 3.3 all-to-all-start.1
  35.5 4.7 gather_fusion.3
  40.2 1.8 all-to-all-done.1
  42.0 4.2 all-to-all-start.2
  47.8 28.6 %all-to-all-done.2 = bf16[8,160,512]{2,1,0:T(8,128)(2,1)S(1)} async-done(((bf16[8,160,512]{2,1,0:T(8,128)(2,1)}), bf16[8,160,512]{2,1,0:T(8,128)(2,1)S(1)}, u32[]{:S(2)}, u32[]{:S(2)}) %all-to-all-start.2) | async-done | bytes 1310752 | tf_op jit(solution)/shard_map/all_to_all | solution.py:67
  77.3 68.1 %while.22 = (s32[]{:T(128)}, f32[10240,128]{1,0:T(8,128)}, s32[10,512]{1,0:T(8,128)S(1)}, bf16[10,512,8]{1,2,0:T(8,128)(2,1)S(1)}, bf16[10,512,128]{2,1,0:T(8,128)(2,1)S(1)}, /*index=5*/s32[]{:T(128)}, s32[]{:T(128)}) while((s32[]{:T(128)}, f32[10240,128]{1,0:T(8,128)}, s32[10,512]{1,0:T(8,128)S(1)}, ...), condition=%wide.region_5.6_spmd.clone, body=%wide.region_4.5_spmd.clone.sunk | while | flops 1351352320 | bytes 13269091 | solution.py:108
  77.9 4.7 convolution_add_fusion.4
  83.2 6.4 %convolution_add_fusion.4 = f32[10240,128]{1,0:T(8,128)} fusion(f32[10240,128]{1,0:T(8,128)} %get-tuple-element.209, bf16[8,512]{1,0:T(8,128)(2,1)S(1)} %dynamic-slice_bitcast_fusion.5, bf16[1280,512]{1,0:T(8,128)(2,1)S(1)} %fusion.68, pred[]{:T(512)S(6)} %compare.30, bf16[10,512,128]{2,1,0:T(8,128)(2,1)S(1)} %get-tuple-element.219, ...), kind=kOutput, calls=%fused_computation.13.clone.1 | convolution fusion | flops 1350041600 | bytes 11935749 | tf_op jit(solution)/shard_map/while/body/eval_jaxpr/dot_general | solution.py:105
  90.2 6.4 %convolution_add_fusion.4 = f32[10240,128]{1,0:T(8,128)} fusion(f32[10240,128]{1,0:T(8,128)} %get-tuple-element.209, bf16[8,512]{1,0:T(8,128)(2,1)S(1)} %dynamic-slice_bitcast_fusion.5, bf16[1280,512]{1,0:T(8,128)(2,1)S(1)} %fusion.68, pred[]{:T(512)S(6)} %compare.30, bf16[10,512,128]{2,1,0:T(8,128)(2,1)S(1)} %get-tuple-element.219, ...), kind=kOutput, calls=%fused_computation.13.clone.1 | convolution fusion | flops 1350041600 | bytes 11935749 | tf_op jit(solution)/shard_map/while/body/eval_jaxpr/dot_general | solution.py:105
  97.2 6.4 %convolution_add_fusion.4 = f32[10240,128]{1,0:T(8,128)} fusion(f32[10240,128]{1,0:T(8,128)} %get-tuple-element.209, bf16[8,512]{1,0:T(8,128)(2,1)S(1)} %dynamic-slice_bitcast_fusion.5, bf16[1280,512]{1,0:T(8,128)(2,1)S(1)} %fusion.68, pred[]{:T(512)S(6)} %compare.30, bf16[10,512,128]{2,1,0:T(8,128)(2,1)S(1)} %get-tuple-element.219, ...), kind=kOutput, calls=%fused_computation.13.clone.1 | convolution fusion | flops 1350041600 | bytes 11935749 | tf_op jit(solution)/shard_map/while/body/eval_jaxpr/dot_general | solution.py:105
  104.1 6.4 %convolution_add_fusion.4 = f32[10240,128]{1,0:T(8,128)} fusion(f32[10240,128]{1,0:T(8,128)} %get-tuple-element.209, bf16[8,512]{1,0:T(8,128)(2,1)S(1)} %dynamic-slice_bitcast_fusion.5, bf16[1280,512]{1,0:T(8,128)(2,1)S(1)} %fusion.68, pred[]{:T(512)S(6)} %compare.30, bf16[10,512,128]{2,1,0:T(8,128)(2,1)S(1)} %get-tuple-element.219, ...), kind=kOutput, calls=%fused_computation.13.clone.1 | convolution fusion | flops 1350041600 | bytes 11935749 | tf_op jit(solution)/shard_map/while/body/eval_jaxpr/dot_general | solution.py:105
  111.1 6.4 %convolution_add_fusion.4 = f32[10240,128]{1,0:T(8,128)} fusion(f32[10240,128]{1,0:T(8,128)} %get-tuple-element.209, bf16[8,512]{1,0:T(8,128)(2,1)S(1)} %dynamic-slice_bitcast_fusion.5, bf16[1280,512]{1,0:T(8,128)(2,1)S(1)} %fusion.68, pred[]{:T(512)S(6)} %compare.30, bf16[10,512,128]{2,1,0:T(8,128)(2,1)S(1)} %get-tuple-element.219, ...), kind=kOutput, calls=%fused_computation.13.clone.1 | convolution fusion | flops 1350041600 | bytes 11935749 | tf_op jit(solution)/shard_map/while/body/eval_jaxpr/dot_general | solution.py:105
  118.1 6.4 %convolution_add_fusion.4 = f32[10240,128]{1,0:T(8,128)} fusion(f32[10240,128]{1,0:T(8,128)} %get-tuple-element.209, bf16[8,512]{1,0:T(8,128)(2,1)S(1)} %dynamic-slice_bitcast_fusion.5, bf16[1280,512]{1,0:T(8,128)(2,1)S(1)} %fusion.68, pred[]{:T(512)S(6)} %compare.30, bf16[10,512,128]{2,1,0:T(8,128)(2,1)S(1)} %get-tuple-element.219, ...), kind=kOutput, calls=%fused_computation.13.clone.1 | convolution fusion | flops 1350041600 | bytes 11935749 | tf_op jit(solution)/shard_map/while/body/eval_jaxpr/dot_general | solution.py:105
  125.1 6.4 %convolution_add_fusion.4 = f32[10240,128]{1,0:T(8,128)} fusion(f32[10240,128]{1,0:T(8,128)} %get-tuple-element.209, bf16[8,512]{1,0:T(8,128)(2,1)S(1)} %dynamic-slice_bitcast_fusion.5, bf16[1280,512]{1,0:T(8,128)(2,1)S(1)} %fusion.68, pred[]{:T(512)S(6)} %compare.30, bf16[10,512,128]{2,1,0:T(8,128)(2,1)S(1)} %get-tuple-element.219, ...), kind=kOutput, calls=%fused_computation.13.clone.1 | convolution fusion | flops 1350041600 | bytes 11935749 | tf_op jit(solution)/shard_map/while/body/eval_jaxpr/dot_general | solution.py:105
  132.1 6.4 %convolution_add_fusion.4 = f32[10240,128]{1,0:T(8,128)} fusion(f32[10240,128]{1,0:T(8,128)} %get-tuple-element.209, bf16[8,512]{1,0:T(8,128)(2,1)S(1)} %dynamic-slice_bitcast_fusion.5, bf16[1280,512]{1,0:T(8,128)(2,1)S(1)} %fusion.68, pred[]{:T(512)S(6)} %compare.30, bf16[10,512,128]{2,1,0:T(8,128)(2,1)S(1)} %get-tuple-element.219, ...), kind=kOutput, calls=%fused_computation.13.clone.1 | convolution fusion | flops 1350041600 | bytes 11935749 | tf_op jit(solution)/shard_map/while/body/eval_jaxpr/dot_general | solution.py:105
  139.0 6.4 %convolution_add_fusion.4 = f32[10240,128]{1,0:T(8,128)} fusion(f32[10240,128]{1,0:T(8,128)} %get-tuple-element.209, bf16[8,512]{1,0:T(8,128)(2,1)S(1)} %dynamic-slice_bitcast_fusion.5, bf16[1280,512]{1,0:T(8,128)(2,1)S(1)} %fusion.68, pred[]{:T(512)S(6)} %compare.30, bf16[10,512,128]{2,1,0:T(8,128)(2,1)S(1)} %get-tuple-element.219, ...), kind=kOutput, calls=%fused_computation.13.clone.1 | convolution fusion | flops 1350041600 | bytes 11935749 | tf_op jit(solution)/shard_map/while/body/eval_jaxpr/dot_general | solution.py:105
  146.5 3.7 convert_element_type.38
  150.2 3.8 all_to_all.41
  155.5 62.8 %all_to_all.55 = bf16[40,8,4096]{2,0,1:T(8,128)(2,1)S(1)} all-to-all(bf16[40,8,4096]{2,0,1:T(8,128)(2,1)S(1)} %copy.147), channel_id=1, replica_groups=mesh['wide'=8,'narrow'=4] {'wide'}, dimensions={1} | all-to-all | bytes 5242880 | tf_op jit(solution)/shard_map/all_to_all | solution.py:110
  218.3 1.5 convolution_convert_fusion.1
  219.8 62.7 %all_to_all.56 = bf16[8,40,4096]{2,1,0:T(8,128)(2,1)S(1)} all-to-all(bf16[8,40,4096]{2,1,0:T(8,128)(2,1)S(1)} %bitcast.147), channel_id=1, replica_groups=mesh['wide'=8,'narrow'=4] {'wide'}, dimensions={0} | all-to-all | bytes 5242880 | tf_op jit(solution)/shard_map/all_to_all | solution.py:114
  284.0 3.2 reshape.167
  287.1 3.9 copy.149
  292.4 67.7 %all-gather.2.cloned.1.call-done = bf16[40,128,8,128]{3,1,2,0:T(8,128)(2,1)} async-done(((bf16[40,32,8,128]{3,1,2,0:T(8,128)(2,1)}), bf16[40,128,8,128]{3,1,2,0:T(8,128)(2,1)}) %all-gather.2.cloned.1.call-update) | async-done | bytes 10485776 | tf_op jit(solution)/shard_map/all_gather | solution.py:121
  360.2 5.5 %convert_bitcast_fusion = bf16[40,32,8,128]{3,1,2,0:T(8,128)(2,1)S(1)} fusion(bf16[40,128,8,128]{3,1,2,0:T(8,128)(2,1)} %all-gather.2.cloned.1.call-done, bf16[128,128]{1,0:T(8,128)(2,1)} %param.27, s32[]{:T(128)S(6)} %select_n.28), kind=kOutput, calls=%fused_computation.27 | convolution fusion | flops 336855040 | bytes 13115396 | tf_op jit(solution)/shard_map/ab,dbrl->darl/dot_general | solution.py:118
  366.9 2.3 convolution_convert_fusion
  369.3 3.8 reshape.169
  373.1 60.6 %while.21 = (s32[]{:T(128)}, f32[10,512,8]{1,2,0:T(8,128)S(1)}, s32[10,512]{1,0:T(8,128)S(1)}, bf16[1280,1024]{1,0:T(8,128)(2,1)S(1)}, bf16[10,512,128]{2,1,0:T(8,128)(2,1)}, /*index=5*/s32[]{:T(128)}) while((s32[]{:T(128)}, f32[10,512,8]{1,2,0:T(8,128)S(1)}, s32[10,512]{1,0:T(8,128)S(1)}, bf16[1280,1024]{1,0:T(8,128)(2,1)S(1)}, ...), condition=%wide.region_7.8_spmd, body=%wide.region_6.7_spmd.sunk | while | flops 1051138 | bytes 5730385 | solution.py:138
  373.2 2.8 gather_fusion
  379.2 2.8 gather_fusion
  385.3 2.8 gather_fusion
  391.4 2.8 gather_fusion
  397.4 2.8 gather_fusion
  403.5 2.8 gather_fusion
  409.5 2.8 gather_fusion
  415.6 2.8 gather_fusion
  421.7 2.8 gather_fusion
  427.7 2.8 gather_fusion
  434.5 5.4 reduce_sum.22
  440.9 5.5 %all-to-all-start.5 = ((f32[8,160,8]{1,2,0:T(8,128)}), f32[8,160,8]{1,2,0:T(8,128)S(1)}, u32[]{:S(2)}, u32[]{:S(2)}) async-start(f32[8,160,8]{1,2,0:T(8,128)} %copy.153), calls=%async_computation.5 | async-start | bytes 131072 | tf_op jit(solution)/shard_map/all_to_all | solution.py:144
  447.1 6.2 %all-to-all-done.5 = f32[8,160,8]{1,2,0:T(8,128)S(1)} async-done(((f32[8,160,8]{1,2,0:T(8,128)}), f32[8,160,8]{1,2,0:T(8,128)S(1)}, u32[]{:S(2)}, u32[]{:S(2)}) %all-to-all-start.5) | async-done | bytes 40992 | tf_op jit(solution)/shard_map/all_to_all | solution.py:144
  454.9 37.9 %all-reduce.3 = (f32[8,8]{0,1:T(8,128)S(1)}, f32[8,8]{1,0:T(8,128)S(1)}) all-reduce(f32[8,8]{0,1:T(8,128)S(1)} %copy-done.8, f32[8,8]{1,0:T(8,128)S(1)} %convolution_bitcast_fusion), channel_id=1, replica_groups=mesh['wide'=8,'narrow'=4] {'wide','narrow'}, use_global_device_ids=true, to_apply=%region_12.14 | all-reduce | flops 128 | bytes 1024 | tf_op jit(solution)/shard_map/psum | solution.py:149
  499.1 40.3 %psum.23 = f32[8,8]{1,0:T(8,128)S(1)} all-reduce(f32[8,8]{1,0:T(8,128)S(1)} %fusion.36), channel_id=1, replica_groups=mesh['wide'=8,'narrow'=4] {'wide','narrow'}, use_global_device_ids=true, to_apply=%region_13.17 | all-reduce | flops 64 | bytes 512 | tf_op jit(solution)/shard_map/psum | solution.py:155
  (188 shorter events, 66.5 us)
Async XLA Ops:
  7.2 211.1 %copy-start = (bf16[320,320]{1,0:T(8,128)(2,1)S(1)}, bf16[320,320]{1,0:T(8,128)(2,1)}, u32[]{:S(2)}) copy-start(bf16[320,320]{1,0:T(8,128)(2,1)} %param.26) | copy-start | bytes 614404
  10.8 0.6 copy-start.11
  14.7 10.6 %copy-start.3 = (f32[8,512]{1,0:T(8,128)S(1)}, f32[8,512]{1,0:T(8,128)}, u32[]{:S(2)}) copy-start(f32[8,512]{1,0:T(8,128)} %param.21) | copy-start | bytes 49156
  17.1 18.3 %copy-start.4 = (bf16[512,4,128]{2,1,0:T(4,128)(2,1)S(1)}, bf16[512,4,128]{2,1,0:T(4,128)(2,1)}, u32[]{:S(2)}) copy-start(bf16[512,4,128]{2,1,0:T(4,128)(2,1)} %param.23) | copy-start | bytes 1572868
  18.0 14.0 %all-to-all-start = ((s32[8,160,4]{1,2,0:T(4,128)}), s32[8,160,4]{1,2,0:T(4,128)S(1)}, u32[]{:S(2)}, u32[]{:S(2)}) async-start(s32[8,160,4]{1,2,0:T(4,128)} %copy.140), calls=%async_computation | async-start | bytes 65536 | tf_op jit(solution)/shard_map/all_to_all | solution.py:81
  32.0 10.0 %all-to-all-start.1 = ((bf16[8,160,8]{1,2,0:T(8,128)(2,1)}), bf16[8,160,8]{1,2,0:T(8,128)(2,1)S(1)}, u32[]{:S(2)}, u32[]{:S(2)}) async-start(bf16[8,160,8]{1,2,0:T(8,128)(2,1)} %copy.143), calls=%async_computation.1 | async-start | bytes 65536 | tf_op jit(solution)/shard_map/all_to_all | solution.py:74
  42.0 34.5 %all-to-all-start.2 = ((bf16[8,160,512]{2,1,0:T(8,128)(2,1)}), bf16[8,160,512]{2,1,0:T(8,128)(2,1)S(1)}, u32[]{:S(2)}, u32[]{:S(2)}) async-start(bf16[8,160,512]{2,1,0:T(8,128)(2,1)} %bitcast.17), calls=%async_computation.2 | async-start | bytes 2621440 | tf_op jit(solution)/shard_map/all_to_all | solution.py:67
  46.1 314.0 %all-gather.2.cloned.1.call-start = ((), (), s32[]{:S(2)}) async-start(), calls=%async_computation.6 | async-start | bytes 13107200 | tf_op jit(solution)/shard_map/all_gather | solution.py:121
  145.4 1.1 copy-start.2
  291.0 0.7 copy-start.6
  365.6 1.3 copy-start.7
  434.5 106.9 %copy-start.1 = (bf16[320,320]{1,0:T(8,128)(2,1)S(1)}, bf16[320,320]{1,0:T(8,128)(2,1)}, u32[]{:S(2)}) copy-start(bf16[320,320]{1,0:T(8,128)(2,1)} %param.26) | copy-start | bytes 614404
  440.0 14.8 %copy-start.10 = (f32[512]{0:T(512)S(1)}, f32[512]{0:T(512)}, u32[]{:S(2)}) copy-start(f32[512]{0:T(512)} %param.22) | copy-start | bytes 6148
  440.0 14.9 %copy-start.8 = (f32[8,8]{0,1:T(8,128)S(1)}, f32[8,8]{0,1:T(8,128)}, u32[]{:S(2)}) copy-start(f32[8,8]{0,1:T(8,128)} %fusion.35) | copy-start | bytes 772
  440.0 100.6 %copy-start.9 = (f32[8,512]{1,0:T(8,128)S(1)}, f32[8,512]{1,0:T(8,128)}, u32[]{:S(2)}) copy-start(f32[8,512]{1,0:T(8,128)} %param.19) | copy-start | bytes 49156
  440.9 12.4 %all-to-all-start.5 = ((f32[8,160,8]{1,2,0:T(8,128)}), f32[8,160,8]{1,2,0:T(8,128)S(1)}, u32[]{:S(2)}, u32[]{:S(2)}) async-start(f32[8,160,8]{1,2,0:T(8,128)} %copy.153), calls=%async_computation.5 | async-start | bytes 131072 | tf_op jit(solution)/shard_map/all_to_all | solution.py:144
  499.0 42.4 %copy-start.5 = (f32[8,512]{1,0:T(8,128)}, f32[8,512]{1,0:T(8,128)S(1)}, u32[]{:S(2)}) copy-start(f32[8,512]{1,0:T(8,128)S(1)} %convolution_subtract_fusion) | copy-start | bytes 49156
Sparse Core Ops, SparseCore 0:
  291.1 68.9 all-gather.1
where the time goes:
time: 550 us; the launch traced here: 548 us
  blocking collectives  204 us (37%)
  waiting for transfers between devices  107 us (19%)
  local copies, waits for them, and re-layouts  95.5 us (17%)
  matrix products  82 us (15%)
  other arithmetic  24.4 us (4%)
  starting transfers between devices  20.4 us (4%)
  between operations  14.4 us (3%)
    all_gather x1, waiting for transfers between devices, on_device(): lax.all_gather(timed_flux, 'narrow', axis=1, tiled=True)  67.7 us
    all_to_all x1, blocking collectives, on_device(): lax.all_to_all(flat_flux, 'wide', split_axis=1, concat_axis=0, tiled=True)  62.8 us
    all_to_all x1, blocking collectives, on_device(): lax.all_to_all(mixed_days, 'wide', split_axis=0, concat_axis=1, tiled=True)  62.7 us
    dot_general x10, matrix products, adjoint_step(): jnp.dot(weighted, foot_block, preferred_element_type=jnp.float32)  62.1 us
    psum x1, blocking collectives, on_device(): lax.psum(gram_matrix(residual_new, residual_new), ('wide', 'narrow'))  40.3 us
    psum x1, blocking collectives, on_device(): lax.psum((gram_matrix(direction, model_image), gram_matrix(residual, resi...  37.9 us
    all_to_all x1, waiting for transfers between devices, on_device(): lax.all_to_all(foot_rows[source].reshape(n_wide, capacity, tile_count * l...  28.6 us
    gather x10, local copies, waits for them, and re-layouts, forward_step(): picked = flux_table[id_block].reshape(rows_block, rhs_count, lon_count)  27.9 us
  transfers between devices with their start and end apart: 5, of which 5 were waited for; matrix products, arithmetic and copies ran while one was open for 2% of the time, Pallas kernels for 0%

commit v1 on v0

--- a/solution.py
+++ b/solution.py
@@ -5,6 +5,28 @@
 from jax.sharding import PartitionSpec as P
 
 HIGHEST = lax.Precision.HIGHEST
+
+
+def laid_out(pieces, dim):
+    pieces = jnp.moveaxis(pieces, 0, dim)
+    lengths = pieces.shape
+    return pieces.reshape(*lengths[:dim], lengths[dim] * lengths[dim + 1], *lengths[dim + 2 :])
+
+
+def gather_around(x, axis, dim):
+    size = lax.axis_size(axis)
+    pairs = [(i, (i + 1) % size) for i in range(size)]
+    back = [(b, a) for a, b in pairs]
+    lower, upper = ([], [])
+    for step in range(size - 1):
+        if step % 2 == 0:
+            lower.append(lax.ppermute(lower[-1] if lower else x, axis, pairs))
+        else:
+            upper.append(lax.ppermute(upper[-1] if upper else x, axis, back))
+    blocks = jnp.stack([*lower[::-1], x, *upper])
+    shift = lax.axis_index(axis) - len(lower)
+    blocks = blocks[(jnp.arange(size) - shift) % size]
+    return laid_out(blocks, dim)
 
 
 def chol_solve(matrix, right):
@@ -118,7 +140,7 @@
     lat_sum = jnp.einsum(
         "ab,dbrl->darl",
         lat_rows,
-        lax.all_gather(timed_flux, "narrow", axis=1, tiled=True),
+        gather_around(timed_flux, "narrow", 1),
         preferred_element_type=jnp.float32,
     )
     spread_lat = lat_sum.astype(jnp.bfloat16)

time: 550 us -> 583 us (1.060)
  local copies, waits for them, and re-layouts: 95.5 us -> 115 us
  waiting for transfers between devices: 107 us -> 123 us
  between operations: 14.4 us -> 0.99 us
  other arithmetic: 24.4 us -> 34.3 us
    ppermute x0 -> x3, waiting for transfers between devices: none -> 83.1 us  [the longest x2 83.1 us: gather_around(): lower.append(lax.ppermute(lower[-1] if lower else x, axis, pairs))]
    all_gather x1 -> x0, waiting for transfers between devices: 67.7 us -> none  [on_device(): lax.all_gather(timed_flux, 'narrow', axis=1, tiled=True)]
    gather x0 -> x8, local copies, waits for them, and re-layouts: none -> 20.9 us
    another operation x2 -> x3, other arithmetic: 1.16 us -> 11 us  [the longest x1 9.87 us: gather_around(): blocks = jnp.stack([*lower[::-1], x, *upper])]
  transfers between devices with their start and end apart: 5 -> 7, of which waited for: 5 -> 6; matrix products, arithmetic and copies ran while one was open for 2% -> 3% of each run, Pallas kernels for 0% -> 0%
where the time goes in v1:
time: 583 us; the launch traced here: 582 us
  blocking collectives  206 us (35%)
  waiting for transfers between devices  123 us (21%)
  local copies, waits for them, and re-layouts  115 us (20%)
  matrix products  82.1 us (14%)
  other arithmetic  34.3 us (6%)
  starting transfers between devices  20.4 us (3%)
    ppermute x2, waiting for transfers between devices, gather_around(): lower.append(lax.ppermute(lower[-1] if lower else x, axis, pairs))  83.1 us
    all_to_all x1, blocking collectives, on_device(): lax.all_to_all(flat_flux, 'wide', split_axis=1, concat_axis=0, tiled=True)  62.7 us
    all_to_all x1, blocking collectives, on_device(): lax.all_to_all(mixed_days, 'wide', split_axis=0, concat_axis=1, tiled=True)  62.7 us
    dot_general x10, matrix products, adjoint_step(): jnp.dot(weighted, foot_block, preferred_element_type=jnp.float32)  62.1 us
    psum x1, blocking collectives, on_device(): lax.psum(gram_matrix(residual_new, residual_new), ('wide', 'narrow'))  40.9 us
    psum x1, blocking collectives, on_device(): lax.psum((gram_matrix(direction, model_image), gram_matrix(residual, resi...  39.5 us
    all_to_all x1, waiting for transfers between devices, on_device(): lax.all_to_all(foot_rows[source].reshape(n_wide, capacity, tile_count * l...  28.7 us
    gather x10, local copies, waits for them, and re-layouts, forward_step(): picked = flux_table[id_block].reshape(rows_block, rhs_count, lon_count)  27.9 us
  transfers between devices with their start and end apart: 7, of which 6 were waited for; matrix products, arithmetic and copies ran while one was open for 3% of the time, Pallas kernels for 0%

profile of v1, /device:TPU:0, one launch (start us, length us, event | category | flops | bytes accessed | tf_op | source)
XLA Modules:
  0.0 581.7 jit_solution(3752493678111787520)
XLA Ops:
  11.5 7.3 %all-to-all-start = ((s32[8,160,4]{1,2,0:T(4,128)}), s32[8,160,4]{1,2,0:T(4,128)S(1)}, u32[]{:S(2)}, u32[]{:S(2)}) async-start(s32[8,160,4]{1,2,0:T(4,128)} %copy.152), calls=%async_computation | async-start | bytes 65536 | tf_op jit(solution)/shard_map/all_to_all | solution.py:103
  19.0 2.8 gather_fusion.2
  22.6 2.9 all-to-all-done
  25.5 3.3 all-to-all-start.1
  29.0 4.7 gather_fusion.3
  35.4 4.2 all-to-all-start.2
  41.3 28.7 %all-to-all-done.2 = bf16[8,160,512]{2,1,0:T(8,128)(2,1)S(1)} async-done(((bf16[8,160,512]{2,1,0:T(8,128)(2,1)}), bf16[8,160,512]{2,1,0:T(8,128)(2,1)S(1)}, u32[]{:S(2)}, u32[]{:S(2)}) %all-to-all-start.2) | async-done | bytes 1310752 | tf_op jit(solution)/shard_map/all_to_all | solution.py:89
  70.8 68.1 %while.24 = (s32[]{:T(128)}, f32[10240,128]{1,0:T(8,128)}, s32[10,512]{1,0:T(8,128)S(1)}, bf16[10,512,8]{1,2,0:T(8,128)(2,1)S(1)}, bf16[10,512,128]{2,1,0:T(8,128)(2,1)S(1)}, /*index=5*/s32[]{:T(128)}, s32[]{:T(128)}) while((s32[]{:T(128)}, f32[10240,128]{1,0:T(8,128)}, s32[10,512]{1,0:T(8,128)S(1)}, ...), condition=%wide.region_5.6_spmd.clone, body=%wide.region_4.5_spmd.clone.sunk | while | flops 1351352320 | bytes 13269091 | solution.py:130
  71.4 4.7 convolution_add_fusion.4
  76.7 6.4 %convolution_add_fusion.4 = f32[10240,128]{1,0:T(8,128)} fusion(f32[10240,128]{1,0:T(8,128)} %get-tuple-element.250, bf16[8,512]{1,0:T(8,128)(2,1)S(1)} %dynamic-slice_bitcast_fusion.5, bf16[1280,512]{1,0:T(8,128)(2,1)S(1)} %fusion.72, pred[]{:T(512)S(6)} %compare.39, bf16[10,512,128]{2,1,0:T(8,128)(2,1)S(1)} %get-tuple-element.260, ...), kind=kOutput, calls=%fused_computation.15.clone.1 | convolution fusion | flops 1350041600 | bytes 11935749 | tf_op jit(solution)/shard_map/while/body/eval_jaxpr/dot_general | solution.py:127
  83.6 6.4 %convolution_add_fusion.4 = f32[10240,128]{1,0:T(8,128)} fusion(f32[10240,128]{1,0:T(8,128)} %get-tuple-element.250, bf16[8,512]{1,0:T(8,128)(2,1)S(1)} %dynamic-slice_bitcast_fusion.5, bf16[1280,512]{1,0:T(8,128)(2,1)S(1)} %fusion.72, pred[]{:T(512)S(6)} %compare.39, bf16[10,512,128]{2,1,0:T(8,128)(2,1)S(1)} %get-tuple-element.260, ...), kind=kOutput, calls=%fused_computation.15.clone.1 | convolution fusion | flops 1350041600 | bytes 11935749 | tf_op jit(solution)/shard_map/while/body/eval_jaxpr/dot_general | solution.py:127
  90.6 6.4 %convolution_add_fusion.4 = f32[10240,128]{1,0:T(8,128)} fusion(f32[10240,128]{1,0:T(8,128)} %get-tuple-element.250, bf16[8,512]{1,0:T(8,128)(2,1)S(1)} %dynamic-slice_bitcast_fusion.5, bf16[1280,512]{1,0:T(8,128)(2,1)S(1)} %fusion.72, pred[]{:T(512)S(6)} %compare.39, bf16[10,512,128]{2,1,0:T(8,128)(2,1)S(1)} %get-tuple-element.260, ...), kind=kOutput, calls=%fused_computation.15.clone.1 | convolution fusion | flops 1350041600 | bytes 11935749 | tf_op jit(solution)/shard_map/while/body/eval_jaxpr/dot_general | solution.py:127
  97.6 6.4 %convolution_add_fusion.4 = f32[10240,128]{1,0:T(8,128)} fusion(f32[10240,128]{1,0:T(8,128)} %get-tuple-element.250, bf16[8,512]{1,0:T(8,128)(2,1)S(1)} %dynamic-slice_bitcast_fusion.5, bf16[1280,512]{1,0:T(8,128)(2,1)S(1)} %fusion.72, pred[]{:T(512)S(6)} %compare.39, bf16[10,512,128]{2,1,0:T(8,128)(2,1)S(1)} %get-tuple-element.260, ...), kind=kOutput, calls=%fused_computation.15.clone.1 | convolution fusion | flops 1350041600 | bytes 11935749 | tf_op jit(solution)/shard_map/while/body/eval_jaxpr/dot_general | solution.py:127
  104.6 6.4 %convolution_add_fusion.4 = f32[10240,128]{1,0:T(8,128)} fusion(f32[10240,128]{1,0:T(8,128)} %get-tuple-element.250, bf16[8,512]{1,0:T(8,128)(2,1)S(1)} %dynamic-slice_bitcast_fusion.5, bf16[1280,512]{1,0:T(8,128)(2,1)S(1)} %fusion.72, pred[]{:T(512)S(6)} %compare.39, bf16[10,512,128]{2,1,0:T(8,128)(2,1)S(1)} %get-tuple-element.260, ...), kind=kOutput, calls=%fused_computation.15.clone.1 | convolution fusion | flops 1350041600 | bytes 11935749 | tf_op jit(solution)/shard_map/while/body/eval_jaxpr/dot_general | solution.py:127
  111.6 6.4 %convolution_add_fusion.4 = f32[10240,128]{1,0:T(8,128)} fusion(f32[10240,128]{1,0:T(8,128)} %get-tuple-element.250, bf16[8,512]{1,0:T(8,128)(2,1)S(1)} %dynamic-slice_bitcast_fusion.5, bf16[1280,512]{1,0:T(8,128)(2,1)S(1)} %fusion.72, pred[]{:T(512)S(6)} %compare.39, bf16[10,512,128]{2,1,0:T(8,128)(2,1)S(1)} %get-tuple-element.260, ...), kind=kOutput, calls=%fused_computation.15.clone.1 | convolution fusion | flops 1350041600 | bytes 11935749 | tf_op jit(solution)/shard_map/while/body/eval_jaxpr/dot_general | solution.py:127
  118.5 6.4 %convolution_add_fusion.4 = f32[10240,128]{1,0:T(8,128)} fusion(f32[10240,128]{1,0:T(8,128)} %get-tuple-element.250, bf16[8,512]{1,0:T(8,128)(2,1)S(1)} %dynamic-slice_bitcast_fusion.5, bf16[1280,512]{1,0:T(8,128)(2,1)S(1)} %fusion.72, pred[]{:T(512)S(6)} %compare.39, bf16[10,512,128]{2,1,0:T(8,128)(2,1)S(1)} %get-tuple-element.260, ...), kind=kOutput, calls=%fused_computation.15.clone.1 | convolution fusion | flops 1350041600 | bytes 11935749 | tf_op jit(solution)/shard_map/while/body/eval_jaxpr/dot_general | solution.py:127
  125.5 6.4 %convolution_add_fusion.4 = f32[10240,128]{1,0:T(8,128)} fusion(f32[10240,128]{1,0:T(8,128)} %get-tuple-element.250, bf16[8,512]{1,0:T(8,128)(2,1)S(1)} %dynamic-slice_bitcast_fusion.5, bf16[1280,512]{1,0:T(8,128)(2,1)S(1)} %fusion.72, pred[]{:T(512)S(6)} %compare.39, bf16[10,512,128]{2,1,0:T(8,128)(2,1)S(1)} %get-tuple-element.260, ...), kind=kOutput, calls=%fused_computation.15.clone.1 | convolution fusion | flops 1350041600 | bytes 11935749 | tf_op jit(solution)/shard_map/while/body/eval_jaxpr/dot_general | solution.py:127
  132.5 6.4 %convolution_add_fusion.4 = f32[10240,128]{1,0:T(8,128)} fusion(f32[10240,128]{1,0:T(8,128)} %get-tuple-element.250, bf16[8,512]{1,0:T(8,128)(2,1)S(1)} %dynamic-slice_bitcast_fusion.5, bf16[1280,512]{1,0:T(8,128)(2,1)S(1)} %fusion.72, pred[]{:T(512)S(6)} %compare.39, bf16[10,512,128]{2,1,0:T(8,128)(2,1)S(1)} %get-tuple-element.260, ...), kind=kOutput, calls=%fused_computation.15.clone.1 | convolution fusion | flops 1350041600 | bytes 11935749 | tf_op jit(solution)/shard_map/while/body/eval_jaxpr/dot_general | solution.py:127
  140.0 3.7 convert_element_type.38
  143.7 3.8 all_to_all.41
  149.0 62.7 %all_to_all.55 = bf16[40,8,4096]{2,0,1:T(8,128)(2,1)S(1)} all-to-all(bf16[40,8,4096]{2,0,1:T(8,128)(2,1)S(1)} %copy.159), channel_id=1, replica_groups=mesh['wide'=8,'narrow'=4] {'wide'}, dimensions={1} | all-to-all | bytes 5242880 | tf_op jit(solution)/shard_map/all_to_all | solution.py:132
  213.3 62.7 %all_to_all.56 = bf16[8,40,4096]{2,1,0:T(8,128)(2,1)S(1)} all-to-all(bf16[8,40,4096]{2,1,0:T(8,128)(2,1)S(1)} %bitcast.159), channel_id=1, replica_groups=mesh['wide'=8,'narrow'=4] {'wide'}, dimensions={0} | all-to-all | bytes 5242880 | tf_op jit(solution)/shard_map/all_to_all | solution.py:136
  277.4 3.2 reshape.220
  282.3 55.9 %collective-permute-done = bf16[40,32,8,128]{3,2,1,0:T(8,128)(2,1)} collective-permute-done((bf16[40,32,8,128]{3,2,1,0:T(8,128)(2,1)}, bf16[40,32,8,128]{3,2,1,0:T(8,128)(2,1)}, u32[]{:S(2)}, u32[]{:S(2)}) %collective-permute-start) | collective-permute-done | bytes 2621472 | tf_op jit(solution)/shard_map/ppermute | solution.py:23
  339.2 3.2 stack_reshape.3
  342.4 27.2 %collective-permute-done.1 = bf16[40,32,8,128]{3,2,1,0:T(8,128)(2,1)} collective-permute-done((bf16[40,32,8,128]{3,2,1,0:T(8,128)(2,1)}, bf16[40,32,8,128]{3,2,1,0:T(8,128)(2,1)}, u32[]{:S(2)}, u32[]{:S(2)}) %collective-permute-start.1) | collective-permute-done | bytes 2621472 | tf_op jit(solution)/shard_map/ppermute | solution.py:23
  369.6 9.9 %pad_maximum_fusion = bf16[4,40,32,8,128]{4,3,2,1,0:T(8,128)(2,1)} fusion(bf16[1,40,32,8,128]{4,3,2,1,0:T(8,128)(2,1)} %bitcast.25, bf16[1,40,32,8,128]{4,3,2,1,0:T(8,128)(2,1)} %stack_reshape.3, bf16[1,40,32,8,128]{4,3,2,1,0:T(8,128)(2,1)} %bitcast.24, bf16[1,40,32,8,128]{4,3,2,1,0:T(8,128)(2,1)} %bitcast.23), kind=kLoop, calls=%fused_computation.28 | loop fusion | flops 15728640 | bytes 20971520 | tf_op jit(solution)/shard_map/stack | solution.py:26
  379.5 20.9 %while.23 = (s32[]{:T(128)}, bf16[4,40,32,8,128]{4,3,2,1,0:T(8,128)(2,1)}, s32[4,1]{0,1:T(1,128)S(1)}, bf16[4,40,32,8,128]{4,3,2,0,1:T(8,128)(2,1)}, s32[]{:T(128)}) while((s32[]{:T(128)}, bf16[4,40,32,8,128]{4,3,2,1,0:T(8,128)(2,1)}, s32[4,1]{0,1:T(1,128)S(1)}, bf16[4,40,32,8,128]{4,3,2,0,1:T(8,128)(2,1)}, s32[]{:T(128)}) %tuple.62), condition=%wide.while_cond, body=%wide.while_body.sunk | while | flops 2 | bytes 5243977 | solution.py:28
  380.1 4.6 bitcast_dynamic-update-slice_fusion.5
  385.3 4.6 bitcast_dynamic-update-slice_fusion.5
  390.5 4.6 bitcast_dynamic-update-slice_fusion.5
  395.7 4.6 bitcast_dynamic-update-slice_fusion.5
  400.4 5.5 convert_bitcast_fusion
  409.5 3.8 reshape.223
  413.3 60.6 %while.22 = (s32[]{:T(128)}, f32[10,512,8]{1,2,0:T(8,128)S(1)}, s32[10,512]{1,0:T(8,128)S(1)}, bf16[1280,1024]{1,0:T(8,128)(2,1)S(1)}, bf16[10,512,128]{2,1,0:T(8,128)(2,1)}, /*index=5*/s32[]{:T(128)}) while((s32[]{:T(128)}, f32[10,512,8]{1,2,0:T(8,128)S(1)}, s32[10,512]{1,0:T(8,128)S(1)}, bf16[1280,1024]{1,0:T(8,128)(2,1)S(1)}, ...), condition=%wide.region_7.8_spmd, body=%wide.region_6.7_spmd.sunk | while | flops 1051138 | bytes 5730385 | solution.py:160
  413.4 2.8 gather_fusion
  419.4 2.8 gather_fusion
  425.5 2.8 gather_fusion
  431.6 2.8 gather_fusion
  437.6 2.8 gather_fusion
  449.8 2.8 gather_fusion
  461.9 2.8 gather_fusion
  467.9 2.8 gather_fusion
  474.7 5.4 reduce_sum.22
  481.1 3.6 all-to-all-start.5
  485.4 6.2 %all-to-all-done.5 = f32[8,160,8]{1,2,0:T(8,128)S(1)} async-done(((f32[8,160,8]{1,2,0:T(8,128)}), f32[8,160,8]{1,2,0:T(8,128)S(1)}, u32[]{:S(2)}, u32[]{:S(2)}) %all-to-all-start.5) | async-done | bytes 40992 | tf_op jit(solution)/shard_map/all_to_all | solution.py:166
  493.1 39.5 %all-reduce.3 = (f32[8,8]{0,1:T(8,128)S(1)}, f32[8,8]{1,0:T(8,128)S(1)}) all-reduce(f32[8,8]{0,1:T(8,128)S(1)} %copy-done.8, f32[8,8]{1,0:T(8,128)S(1)} %convolution_bitcast_fusion), channel_id=1, replica_groups=mesh['wide'=8,'narrow'=4] {'wide','narrow'}, use_global_device_ids=true, to_apply=%region_12.14 | all-reduce | flops 128 | bytes 1024 | tf_op jit(solution)/shard_map/psum | solution.py:171
  538.9 40.9 %psum.23 = f32[8,8]{1,0:T(8,128)S(1)} all-reduce(f32[8,8]{1,0:T(8,128)S(1)} %fusion.41), channel_id=1, replica_groups=mesh['wide'=8,'narrow'=4] {'wide','narrow'}, use_global_device_ids=true, to_apply=%region_13.17 | all-reduce | flops 64 | bytes 512 | tf_op jit(solution)/shard_map/psum | solution.py:177
  (203 shorter events, 86.2 us)
Async XLA Ops:
  0.6 211.1 %copy-start = (bf16[320,320]{1,0:T(8,128)(2,1)S(1)}, bf16[320,320]{1,0:T(8,128)(2,1)}, u32[]{:S(2)}) copy-start(bf16[320,320]{1,0:T(8,128)(2,1)} %param.26) | copy-start | bytes 614404
  4.2 0.6 copy-start.11
  8.2 10.6 %copy-start.3 = (f32[8,512]{1,0:T(8,128)S(1)}, f32[8,512]{1,0:T(8,128)}, u32[]{:S(2)}) copy-start(f32[8,512]{1,0:T(8,128)} %param.21) | copy-start | bytes 49156
  10.5 18.3 %copy-start.4 = (bf16[512,4,128]{2,1,0:T(4,128)(2,1)S(1)}, bf16[512,4,128]{2,1,0:T(4,128)(2,1)}, u32[]{:S(2)}) copy-start(bf16[512,4,128]{2,1,0:T(4,128)(2,1)} %param.23) | copy-start | bytes 1572868
  11.5 14.0 %all-to-all-start = ((s32[8,160,4]{1,2,0:T(4,128)}), s32[8,160,4]{1,2,0:T(4,128)S(1)}, u32[]{:S(2)}, u32[]{:S(2)}) async-start(s32[8,160,4]{1,2,0:T(4,128)} %copy.152), calls=%async_computation | async-start | bytes 65536 | tf_op jit(solution)/shard_map/all_to_all | solution.py:103
  25.5 10.0 %all-to-all-start.1 = ((bf16[8,160,8]{1,2,0:T(8,128)(2,1)}), bf16[8,160,8]{1,2,0:T(8,128)(2,1)S(1)}, u32[]{:S(2)}, u32[]{:S(2)}) async-start(bf16[8,160,8]{1,2,0:T(8,128)(2,1)} %copy.155), calls=%async_computation.1 | async-start | bytes 65536 | tf_op jit(solution)/shard_map/all_to_all | solution.py:96
  35.4 34.5 %all-to-all-start.2 = ((bf16[8,160,512]{2,1,0:T(8,128)(2,1)}), bf16[8,160,512]{2,1,0:T(8,128)(2,1)S(1)}, u32[]{:S(2)}, u32[]{:S(2)}) async-start(bf16[8,160,512]{2,1,0:T(8,128)(2,1)} %bitcast.17), calls=%async_computation.2 | async-start | bytes 2621440 | tf_op jit(solution)/shard_map/all_to_all | solution.py:89
  138.9 1.1 copy-start.2
  277.4 61.1 %copy-start.6 = (f32[8,512]{1,0:T(8,128)S(1)}, f32[8,512]{1,0:T(8,128)}, u32[]{:S(2)}) copy-start(f32[8,512]{1,0:T(8,128)} %param.20) | copy-start | bytes 49156
  280.6 57.6 %collective-permute-start = (bf16[40,32,8,128]{3,2,1,0:T(8,128)(2,1)}, bf16[40,32,8,128]{3,2,1,0:T(8,128)(2,1)}, u32[]{:S(2)}, u32[]{:S(2)}) collective-permute-start(bf16[40,32,8,128]{3,2,1,0:T(8,128)(2,1)} %reshape.220), channel_id=1, source_target_pairs={{0,1},{1,2},{2,3},{3,0},{4,5},{5,6},{6,7},{7,4},{8,9},{9,10},{10,1... | collective-permute-start | bytes 7864328 | tf_op jit(solution)/shard_map/ppermute | solution.py:23
  280.6 61.8 %collective-permute-start.2 = (bf16[40,32,8,128]{3,2,1,0:T(8,128)(2,1)}, bf16[40,32,8,128]{3,2,1,0:T(8,128)(2,1)}, u32[]{:S(2)}, u32[]{:S(2)}) collective-permute-start(bf16[40,32,8,128]{3,2,1,0:T(8,128)(2,1)} %reshape.220), channel_id=1, source_target_pairs={{1,0},{2,1},{3,2},{0,3},{5,4},{6,5},{7,6},{4,7},{9,8},{10,9},{11,1... | collective-permute-start | bytes 7864328 | tf_op jit(solution)/shard_map/ppermute | solution.py:25
  338.2 31.4 %collective-permute-start.1 = (bf16[40,32,8,128]{3,2,1,0:T(8,128)(2,1)}, bf16[40,32,8,128]{3,2,1,0:T(8,128)(2,1)}, u32[]{:S(2)}, u32[]{:S(2)}) collective-permute-start(bf16[40,32,8,128]{3,2,1,0:T(8,128)(2,1)} %collective-permute-done), channel_id=1, source_target_pairs={{0,1},{1,2},{2,3},{3,0},{4,5},{5,6},{6,7},{7,4},{8,9},{9,10},{10,1... | collective-permute-start | bytes 7864328 | tf_op jit(solution)/shard_map/ppermute | solution.py:23
  405.9 1.3 copy-start.7
  474.7 107.0 %copy-start.1 = (bf16[320,320]{1,0:T(8,128)(2,1)S(1)}, bf16[320,320]{1,0:T(8,128)(2,1)}, u32[]{:S(2)}) copy-start(bf16[320,320]{1,0:T(8,128)(2,1)} %param.26) | copy-start | bytes 614404
  480.2 12.8 %copy-start.10 = (f32[512]{0:T(512)S(1)}, f32[512]{0:T(512)}, u32[]{:S(2)}) copy-start(f32[512]{0:T(512)} %param.22) | copy-start | bytes 6148
  480.2 12.9 %copy-start.8 = (f32[8,8]{0,1:T(8,128)S(1)}, f32[8,8]{0,1:T(8,128)}, u32[]{:S(2)}) copy-start(f32[8,8]{0,1:T(8,128)} %fusion.40) | copy-start | bytes 772
  480.2 100.7 %copy-start.9 = (f32[8,512]{1,0:T(8,128)S(1)}, f32[8,512]{1,0:T(8,128)}, u32[]{:S(2)}) copy-start(f32[8,512]{1,0:T(8,128)} %param.19) | copy-start | bytes 49156
  481.1 10.4 %all-to-all-start.5 = ((f32[8,160,8]{1,2,0:T(8,128)}), f32[8,160,8]{1,2,0:T(8,128)S(1)}, u32[]{:S(2)}, u32[]{:S(2)}) async-start(f32[8,160,8]{1,2,0:T(8,128)} %copy.167), calls=%async_computation.5 | async-start | bytes 131072 | tf_op jit(solution)/shard_map/all_to_all | solution.py:166
  538.7 43.0 %copy-start.5 = (f32[8,512]{1,0:T(8,128)}, f32[8,512]{1,0:T(8,128)S(1)}, u32[]{:S(2)}) copy-start(f32[8,512]{1,0:T(8,128)S(1)} %convolution_subtract_fusion) | copy-start | bytes 49156
